TPU v7x, 32 devices: a whole 2x2x4 slice. The times are simulated.
32 devices in a mesh: row: 4 (over z), col: 4 (over y, core), ch: 2 (over x).
Axes of the slice: x: 2, y: 2, z: 4, core: 2. Of those that a mesh axis runs over, the one named last changes fastest.
Arguments:
- spectra: float32 [384, 128, 1024], P('ch', 'row', 'col'), may hold values from 0 to 1
- pixel_factor: float32 [64, 128, 1024], P(None, 'row', 'col'), may hold values from 0.1 to 1
- channel_factor: float32 [64, 384], P(None, 'ch'), may hold values from 0.1 to 1
- labels: int32 [128, 1024], P('row', 'col'), may hold values from 0 to 3
Outputs:
- smoothed_factor: float32 [64, 128, 1024], P(None, 'row', 'col')
- new_channel: float32 [64, 384], P(None, 'ch')
All inputs are finite; a program needn't handle non-finite values.
Results may differ from a plain program's by a relative error of at most 0.000068.
Values sent between devices are 32-bit elements; how exact they have to be, the bound alone decides.
A program may use at most 64 MiB of HBM per device.

v0:
```python
import jax
import jax.numpy as jnp
from jax import lax
from jax.sharding import PartitionSpec as P

SMOOTH = 3
epsilon = 1e-09


def padded_2(block, sides, width):
    for axis, dim in sides:
        count = lax.axis_size(axis)
        forward = [(i, i + 1) for i in range(count - 1)]
        backward = [(target, source) for source, target in forward]
        low = lax.ppermute(
            lax.slice_in_dim(block, block.shape[dim] - width, None, axis=dim), axis, forward
        )
        high = lax.ppermute(lax.slice_in_dim(block, 0, width, axis=dim), axis, backward)
        block = jnp.concatenate([low, block, high], axis=dim)
    return block


def coefficients(marked):
    center = marked[1:-1, 1:-1]
    result = []
    for neighbour in (marked[:-2, 1:-1], marked[2:, 1:-1], marked[1:-1, :-2], marked[1:-1, 2:]):
        result.append(
            jnp.where(neighbour == 0, 0.0, jnp.where(neighbour == center, 1.0, 0.25)).astype(
                jnp.float32
            )
        )
    return result


def smooth_once(padded, field, weights):
    combined = field + weights[0] * padded[:, :-2, 1:-1] + weights[1] * padded[:, 2:, 1:-1]
    combined = combined + weights[2] * padded[:, 1:-1, :-2] + weights[3] * padded[:, 1:-1, 2:]
    return combined / (1.0 + weights[0] + weights[1] + weights[2] + weights[3])


def lift_factor(own_factor, pixel_top, chan_gram):
    factor_rank = own_factor.shape[0]
    flat_own = own_factor.reshape(factor_rank, -1)
    lower = jnp.dot(
        chan_gram, flat_own, precision=lax.Precision.HIGHEST, preferred_element_type=jnp.float32
    )
    return (flat_own * pixel_top.reshape(factor_rank, -1) / (lower + epsilon)).reshape(
        own_factor.shape
    )


def shards(spectra, pixel_factor, channel_factor, labels):
    precise = lax.Precision.HIGHEST
    contraction = (((1,), (1,)), ((), ()))
    factor_rank, row_count, col_count = pixel_factor.shape
    flat_pixel = pixel_factor.reshape(factor_rank, row_count * col_count)
    flat_data = spectra.reshape(spectra.shape[0], row_count * col_count)
    chan_top = lax.dot_general(
        flat_pixel, flat_data, contraction, precision=precise, preferred_element_type=jnp.float32
    )
    pixel_gram = lax.dot_general(
        flat_pixel, flat_pixel, contraction, precision=precise, preferred_element_type=jnp.float32
    )
    chan_top, pixel_gram = lax.psum((chan_top, pixel_gram), ("row", "col"))
    new_channel = (
        channel_factor
        * chan_top
        / (
            jnp.dot(
                pixel_gram, channel_factor, precision=precise, preferred_element_type=jnp.float32
            )
            + epsilon
        )
    )
    part_top = jnp.dot(
        new_channel, flat_data, precision=precise, preferred_element_type=jnp.float32
    ).reshape(factor_rank, row_count, col_count)
    part_gram = lax.dot_general(
        new_channel, new_channel, contraction, precision=precise, preferred_element_type=jnp.float32
    )
    marked = labels + 1
    share_rows = row_count // lax.axis_size("ch")
    share_start = lax.axis_index("ch") * share_rows
    pixel_top = lax.psum_scatter(part_top, "ch", scatter_dimension=1, tiled=True)
    chan_gram = lax.psum(part_gram, "ch")
    own_factor = lax.dynamic_slice_in_dim(pixel_factor, share_start, share_rows, 1)
    own_marks = lax.dynamic_slice_in_dim(marked, share_start, share_rows, 0)
    field = lift_factor(own_factor, pixel_top, chan_gram)
    border_marks = padded_2(own_marks, ((("row", "ch"), 0), ("col", 1)), 1)
    weights = coefficients(border_marks)
    for iteration in range(SMOOTH):
        padded = padded_2(field, ((("row", "ch"), 1), ("col", 2)), 1)
        field = smooth_once(padded, field, weights)
    smoothed_factor = lax.all_gather(field, "ch", axis=1, tiled=True)
    return (smoothed_factor, new_channel)


def solution(mesh):
    placed = (P("ch", "row", "col"), P(None, "row", "col"), P(None, "ch"), P("row", "col"))
    return jax.shard_map(
        shards,
        mesh=mesh,
        in_specs=placed,
        out_specs=(P(None, "row", "col"), P(None, "ch")),
        check_vma=False,
    )
```

profile of v0, /device:TPU:0, one launch (start us, length us, event | category | flops | bytes accessed | tf_op | source)
XLA Modules:
  0.0 290.6 jit_solution(9528814193666715446)
XLA Ops:
  7.2 7.0 %fusion.42 = f32[64,64]{1,0:T(8,128)} fusion(f32[64,32,256]{2,1,0:T(8,128)} %param.5), kind=kOutput, calls=%fused_computation.64 | convolution fusion | flops 402653184 | bytes 2113536 | tf_op jit(solution)/shard_map/dot_general | solution.py:61
  14.2 12.2 %fusion.36 = f32[64,192]{1,0:T(8,128)} fusion(f32[192,32,256]{2,1,0:T(8,128)} %param.4, f32[64,32,256]{2,1,0:T(8,128)S(1)} %copy-done.2), kind=kOutput, calls=%fused_computation.61 | convolution fusion | flops 1207959552 | bytes 8437760 | tf_op jit(solution)/shard_map/dot_general | solution.py:58
  26.5 0.2 reduce-scatter.2.cloned.1.call-start
  26.7 91.5 %all-reduce.3.cloned.1.call-done = (f32[64,64]{1,0:T(8,128)}, f32[64,192]{1,0:T(8,128)}) async-done(((f32[64,64]{1,0:T(8,128)}, f32[64,192]{1,0:T(8,128)}), (f32[64,64]{1,0:T(8,128)}, f32[64,192]{1,0:T(8,128)})) %all-reduce.3.cloned.1.call-update) | async-done | bytes 65552 | tf_op jit(solution)/shard_map/psum | solution.py:64
  118.2 1.1 fusion.41
  119.3 11.4 %fusion = f32[64,32,256]{2,0,1:T(8,128)} fusion(f32[64,192]{1,0:T(8,128)S(1)} %fusion.41, f32[24,8,32,256]{3,2,1,0:T(8,128)} %bitcast.30), kind=kOutput, calls=%fused_computation | convolution fusion | flops 1207959552 | bytes 8437760 | tf_op jit(solution)/shard_map/dot_general | solution.py:75
  130.8 0.7 copy-done.4
  131.5 1.3 collective-permute-start.2
  132.8 4.5 %collective-permute-start = (s32[1,256]{1,0:T(1,128)S(1)}, s32[1,256]{1,0:T(1,128)S(1)}, u32[]{:S(2)}, u32[]{:S(2)}) collective-permute-start(s32[1,256]{1,0:T(1,128)S(1)} %get-tuple-element.34), channel_id=1, source_target_pairs={{0,1},{1,8},{8,9},{9,16},{16,17},{17,24},{24,25},{2,3},{3,10},{10,... | collective-permute-start | bytes 3080 | tf_op jit(solution)/shard_map/ppermute | solution.py:15
  137.4 0.6 copy.164
  138.0 0.6 collective-permute-done
  138.6 0.2 fusion.55
  138.8 10.2 %psum.23 = f32[64,64]{1,0:T(8,128)S(1)} all-reduce(f32[64,64]{1,0:T(8,128)S(1)} %fusion.55), channel_id=1, replica_groups=mesh['row'=4,'col'=4,'ch'=2] {'ch'}, use_global_device_ids=true, to_apply=%region_3.0 | all-reduce | flops 4096 | bytes 32768 | tf_op jit(solution)/shard_map/psum | solution.py:85
  149.0 13.5 %reduce-scatter.2.cloned.1.call-done = f32[64,16,256]{2,0,1:T(8,128)} async-done(((f32[64,32,256]{2,0,1:T(8,128)}), f32[64,16,256]{2,0,1:T(8,128)}) %reduce-scatter.2.cloned.1.call-update) | async-done | bytes 1048592 | tf_op jit(solution)/shard_map/reduce_scatter | solution.py:84
  162.5 1.3 copy.163
  163.8 1.1 fusion.5
  165.0 0.3 copy.166
  165.4 1.3 collective-permute-start.3
  166.7 4.5 %collective-permute-start.1 = (f32[64,1,256]{2,0,1:T(8,128)S(1)}, f32[64,1,256]{2,0,1:T(8,128)S(1)}, u32[]{:S(2)}, u32[]{:S(2)}) collective-permute-start(f32[64,1,256]{2,0,1:T(8,128)S(1)} %copy.160), channel_id=1, source_target_pairs={{0,1},{1,8},{8,9},{9,16},{16,17},{17,24},{24,25},{2,3},{3,10},{10,... | collective-permute-start | bytes 196616 | tf_op jit(solution)/shard_map/ppermute | solution.py:15
  171.4 1.3 collective-permute-start.6
  172.7 3.0 %collective-permute-start.4 = (s32[18,1]{1,0:T(8,128)S(1)}, s32[18,1]{1,0:T(8,128)S(1)}, u32[]{:S(2)}, u32[]{:S(2)}) collective-permute-start(s32[18,1]{1,0:T(8,128)S(1)} %get-tuple-element.32), channel_id=1, source_target_pairs={{0,2},{2,4},{4,6},{1,3},{3,5},{5,7},{8,10},{10,12},{12,14},{9,11},... | collective-permute-start | bytes 224 | tf_op jit(solution)/shard_map/ppermute | solution.py:15
  175.7 1.6 copy.135
  177.5 3.0 %collective-permute-start.5 = (f32[64,18,1]{0,1,2:T(8,128)S(1)}, f32[64,18,1]{0,1,2:T(8,128)S(1)}, u32[]{:S(2)}, u32[]{:S(2)}) collective-permute-start(f32[64,18,1]{0,1,2:T(8,128)S(1)} %get-tuple-element.23), channel_id=1, source_target_pairs={{0,2},{2,4},{4,6},{1,3},{3,5},{5,7},{8,10},{10,12},{12,14},{9,11},... | collective-permute-start | bytes 13832 | tf_op jit(solution)/shard_map/ppermute | solution.py:15
  180.5 1.5 collective-permute-start.7
  182.2 0.1 copy.145
  182.7 0.9 collective-permute-done.7
  183.6 9.2 %fusion.26 = f32[64,16,256]{0,1,2:T(8,128)S(1)} fusion(f32[64,18,1]{0,1,2:T(8,128)S(1)} %collective-permute-done.7, f32[64,1,256]{0,1,2:T(1,128)S(1)} %copy.139, f32[64,16,256]{0,1,2:T(8,128)} %copy-done.1, f32[64,1,256]{0,1,2:T(1,128)S(1)} %copy.133, f32[64,18,1]{0,1,2:T(8,128)S(1)} %collective-permute-done.5, f32[16,256]{0,1:T(8,128)S(1)} %copy.145, ...), kind=kLoop, calls=%fused_computation.44 | loop fusion | flops 4456448 | bytes 2319360 | tf_op jit(solution)/shard_map/div | solution.py:38
  192.8 0.2 fusion.51
  193.1 1.3 collective-permute-start.9
  194.5 4.5 %collective-permute-start.8 = (f32[64,1,256]{2,0,1:T(8,128)S(1)}, f32[64,1,256]{2,0,1:T(8,128)S(1)}, u32[]{:S(2)}, u32[]{:S(2)}) collective-permute-start(f32[64,1,256]{2,0,1:T(8,128)S(1)} %copy.146), channel_id=1, source_target_pairs={{0,1},{1,8},{8,9},{9,16},{16,17},{17,24},{24,25},{2,3},{3,10},{10,... | collective-permute-start | bytes 196616 | tf_op jit(solution)/shard_map/ppermute | solution.py:15
  199.0 0.2 collective-permute-done.9
  199.4 2.0 collective-permute-done.8
  201.4 2.8 collective-permute-start.10
  204.3 1.3 collective-permute-start.11
  205.6 2.4 collective-permute-done.11
  208.0 9.2 %fusion.17 = f32[64,16,256]{0,1,2:T(8,128)S(1)} fusion(f32[64,18,1]{0,1,2:T(8,128)S(1)} %collective-permute-done.11, f32[64,1,256]{0,1,2:T(1,128)S(1)} %copy.149, f32[64,16,256]{0,1,2:T(8,128)} %copy-done, f32[64,1,256]{0,1,2:T(1,128)S(1)} %copy.147, f32[64,18,1]{0,1,2:T(8,128)S(1)} %collective-permute-done.10, f32[16,256]{0,1:T(8,128)S(1)} %copy.145, ...), kind=kLoop, calls=%fused_computation.27 | loop fusion | flops 4456448 | bytes 2319360 | tf_op jit(solution)/shard_map/div | solution.py:38
  217.2 0.2 fusion.50
  217.5 1.3 collective-permute-start.13
  218.9 4.9 %collective-permute-start.12 = (f32[64,1,256]{2,0,1:T(8,128)S(1)}, f32[64,1,256]{2,0,1:T(8,128)S(1)}, u32[]{:S(2)}, u32[]{:S(2)}) collective-permute-start(f32[64,1,256]{2,0,1:T(8,128)S(1)} %copy.152), channel_id=1, source_target_pairs={{0,1},{1,8},{8,9},{9,16},{16,17},{17,24},{24,25},{2,3},{3,10},{10,... | collective-permute-start | bytes 196616 | tf_op jit(solution)/shard_map/ppermute | solution.py:15
  223.8 0.2 collective-permute-done.13
  224.1 1.6 collective-permute-done.12
  225.8 3.6 %collective-permute-start.14 = (f32[64,18,1]{0,1,2:T(8,128)S(1)}, f32[64,18,1]{0,1,2:T(8,128)S(1)}, u32[]{:S(2)}, u32[]{:S(2)}) collective-permute-start(f32[64,18,1]{0,1,2:T(8,128)S(1)} %get-tuple-element.19), channel_id=1, source_target_pairs={{0,2},{2,4},{4,6},{1,3},{3,5},{5,7},{8,10},{10,12},{12,14},{9,11},... | collective-permute-start | bytes 13832 | tf_op jit(solution)/shard_map/ppermute | solution.py:15
  229.4 1.3 collective-permute-start.15
  230.7 2.1 collective-permute-done.15
  232.7 5.2 %fusion.8 = f32[64,16,256]{0,1,2:T(8,128)} fusion(f32[64,18,1]{0,1,2:T(8,128)S(1)} %collective-permute-done.15, f32[64,1,256]{0,1,2:T(1,128)S(1)} %copy.155, f32[64,16,256]{0,1,2:T(8,128)S(1)} %fusion.17, f32[64,1,256]{0,1,2:T(1,128)S(1)} %copy.153, f32[64,18,1]{0,1,2:T(8,128)S(1)} %collective-permute-done.14, f32[16,256]{0,1:T(8,128)S(1)} %copy.145, ...), kind=kLoop, calls=%fused_computation.10 | loop fusion | flops 4456448 | bytes 2319360 | tf_op jit(solution)/shard_map/div | solution.py:38
  237.9 3.5 %copy.158 = f32[64,16,256]{2,0,1:T(8,128)} copy(f32[64,16,256]{0,1,2:T(8,128)} %fusion.8) | data formatting | bytes 2097152 | tf_op jit(solution)/shard_map/div | solution.py:38
  241.4 38.5 %all-gather.2.cloned.1.call-done = f32[64,32,256]{2,0,1:T(8,128)} async-done(((f32[64,16,256]{2,0,1:T(8,128)}), f32[64,32,256]{2,0,1:T(8,128)}) %all-gather.2.cloned.1.call-update) | async-done | bytes 2097168 | tf_op jit(solution)/shard_map/all_gather | solution.py:94
  280.0 4.1 %copy.159 = f32[64,32,256]{2,1,0:T(8,128)} copy(f32[64,32,256]{2,0,1:T(8,128)} %all-gather.2.cloned.1.call-done) | data formatting | bytes 4194304
  (50 shorter events, 1.9 us)
Async XLA Ops:
  7.2 7.1 %copy-start.2 = (f32[64,32,256]{2,1,0:T(8,128)S(1)}, f32[64,32,256]{2,1,0:T(8,128)}, u32[]{:S(2)}) copy-start(f32[64,32,256]{2,1,0:T(8,128)} %param.5) | copy-start | bytes 6291460
  7.2 111.1 %all-reduce.3.cloned.1.call-start = ((), (), s32[]{:S(2)}) async-start(), calls=%async_computation.3 | async-start | bytes 196608 | tf_op jit(solution)/shard_map/psum | solution.py:64
  14.2 104.0 %copy-start.5 = (f32[64,192]{1,0:T(8,128)S(1)}, f32[64,192]{1,0:T(8,128)}, u32[]{:S(2)}) copy-start(f32[64,192]{1,0:T(8,128)} %param.6) | copy-start | bytes 147460
  26.5 136.1 %reduce-scatter.2.cloned.1.call-start = ((), (), s32[]{:S(2)}) async-start(), calls=%async_computation.1 | async-start | bytes 3145728 | tf_op jit(solution)/shard_map/reduce_scatter | solution.py:84
  119.3 19.3 %copy-start.3 = (f32[64,192]{1,0:T(8,128)}, f32[64,192]{1,0:T(8,128)S(1)}, u32[]{:S(2)}) copy-start(f32[64,192]{1,0:T(8,128)S(1)} %fusion.41) | copy-start | bytes 147460
  130.7 0.8 copy-start.4
  130.7 149.3 %all-gather.2.cloned.1.call-start = ((), (), s32[]{:S(2)}) async-start(), calls=%async_computation.2 | async-start | bytes 3145728 | tf_op jit(solution)/shard_map/all_gather | solution.py:94
  131.5 6.6 %collective-permute-start.2 = (s32[1,256]{1,0:T(1,128)S(1)}, s32[1,256]{1,0:T(1,128)S(1)}, u32[]{:S(2)}, u32[]{:S(2)}) collective-permute-start(s32[1,256]{1,0:T(1,128)S(1)} %get-tuple-element.33), channel_id=1, source_target_pairs={{1,0},{8,1},{9,8},{16,9},{17,16},{24,17},{25,24},{3,2},{10,3},{11,... | collective-permute-start | bytes 3080 | tf_op jit(solution)/shard_map/ppermute | solution.py:18
  132.8 5.8 %collective-permute-start = (s32[1,256]{1,0:T(1,128)S(1)}, s32[1,256]{1,0:T(1,128)S(1)}, u32[]{:S(2)}, u32[]{:S(2)}) collective-permute-start(s32[1,256]{1,0:T(1,128)S(1)} %get-tuple-element.34), channel_id=1, source_target_pairs={{0,1},{1,8},{8,9},{9,16},{16,17},{17,24},{24,25},{2,3},{3,10},{10,... | collective-permute-start | bytes 3080 | tf_op jit(solution)/shard_map/ppermute | solution.py:15
  165.4 11.9 %collective-permute-start.3 = (f32[64,1,256]{2,0,1:T(8,128)S(1)}, f32[64,1,256]{2,0,1:T(8,128)S(1)}, u32[]{:S(2)}, u32[]{:S(2)}) collective-permute-start(f32[64,1,256]{2,0,1:T(8,128)S(1)} %copy.161), channel_id=1, source_target_pairs={{1,0},{8,1},{9,8},{16,9},{17,16},{24,17},{25,24},{3,2},{10,3},{11,... | collective-permute-start | bytes 196616 | tf_op jit(solution)/shard_map/ppermute | solution.py:18
  166.7 10.7 %collective-permute-start.1 = (f32[64,1,256]{2,0,1:T(8,128)S(1)}, f32[64,1,256]{2,0,1:T(8,128)S(1)}, u32[]{:S(2)}, u32[]{:S(2)}) collective-permute-start(f32[64,1,256]{2,0,1:T(8,128)S(1)} %copy.160), channel_id=1, source_target_pairs={{0,1},{1,8},{8,9},{9,16},{16,17},{17,24},{24,25},{2,3},{3,10},{10,... | collective-permute-start | bytes 196616 | tf_op jit(solution)/shard_map/ppermute | solution.py:15
  171.4 10.7 %collective-permute-start.6 = (s32[18,1]{1,0:T(8,128)S(1)}, s32[18,1]{1,0:T(8,128)S(1)}, u32[]{:S(2)}, u32[]{:S(2)}) collective-permute-start(s32[18,1]{1,0:T(8,128)S(1)} %get-tuple-element.31), channel_id=1, source_target_pairs={{2,0},{4,2},{6,4},{3,1},{5,3},{7,5},{10,8},{12,10},{14,12},{11,9},... | collective-permute-start | bytes 224 | tf_op jit(solution)/shard_map/ppermute | solution.py:18
  172.7 9.4 %collective-permute-start.4 = (s32[18,1]{1,0:T(8,128)S(1)}, s32[18,1]{1,0:T(8,128)S(1)}, u32[]{:S(2)}, u32[]{:S(2)}) collective-permute-start(s32[18,1]{1,0:T(8,128)S(1)} %get-tuple-element.32), channel_id=1, source_target_pairs={{0,2},{2,4},{4,6},{1,3},{3,5},{5,7},{8,10},{10,12},{12,14},{9,11},... | collective-permute-start | bytes 224 | tf_op jit(solution)/shard_map/ppermute | solution.py:15
  177.3 5.4 %copy-start.1 = (f32[64,16,256]{0,1,2:T(8,128)}, f32[64,16,256]{0,1,2:T(8,128)S(1)}, u32[]{:S(2)}) copy-start(f32[64,16,256]{0,1,2:T(8,128)S(1)} %copy.135) | copy-start | bytes 3145732
  177.5 5.1 %collective-permute-start.5 = (f32[64,18,1]{0,1,2:T(8,128)S(1)}, f32[64,18,1]{0,1,2:T(8,128)S(1)}, u32[]{:S(2)}, u32[]{:S(2)}) collective-permute-start(f32[64,18,1]{0,1,2:T(8,128)S(1)} %get-tuple-element.23), channel_id=1, source_target_pairs={{0,2},{2,4},{4,6},{1,3},{3,5},{5,7},{8,10},{10,12},{12,14},{9,11},... | collective-permute-start | bytes 13832 | tf_op jit(solution)/shard_map/ppermute | solution.py:15
  180.5 3.1 %collective-permute-start.7 = (f32[64,18,1]{0,1,2:T(8,128)S(1)}, f32[64,18,1]{0,1,2:T(8,128)S(1)}, u32[]{:S(2)}, u32[]{:S(2)}) collective-permute-start(f32[64,18,1]{0,1,2:T(8,128)S(1)} %get-tuple-element.24), channel_id=1, source_target_pairs={{2,0},{4,2},{6,4},{3,1},{5,3},{7,5},{10,8},{12,10},{14,12},{11,9},... | collective-permute-start | bytes 13832 | tf_op jit(solution)/shard_map/ppermute | solution.py:18
  192.8 12.8 %copy-start = (f32[64,16,256]{0,1,2:T(8,128)}, f32[64,16,256]{0,1,2:T(8,128)S(1)}, u32[]{:S(2)}) copy-start(f32[64,16,256]{0,1,2:T(8,128)S(1)} %fusion.26) | copy-start | bytes 3145732
  193.1 6.2 %collective-permute-start.9 = (f32[64,1,256]{2,0,1:T(8,128)S(1)}, f32[64,1,256]{2,0,1:T(8,128)S(1)}, u32[]{:S(2)}, u32[]{:S(2)}) collective-permute-start(f32[64,1,256]{2,0,1:T(8,128)S(1)} %copy.148), channel_id=1, source_target_pairs={{1,0},{8,1},{9,8},{16,9},{17,16},{24,17},{25,24},{3,2},{10,3},{11,... | collective-permute-start | bytes 196616 | tf_op jit(solution)/shard_map/ppermute | solution.py:18
  194.5 6.8 %collective-permute-start.8 = (f32[64,1,256]{2,0,1:T(8,128)S(1)}, f32[64,1,256]{2,0,1:T(8,128)S(1)}, u32[]{:S(2)}, u32[]{:S(2)}) collective-permute-start(f32[64,1,256]{2,0,1:T(8,128)S(1)} %copy.146), channel_id=1, source_target_pairs={{0,1},{1,8},{8,9},{9,16},{16,17},{17,24},{24,25},{2,3},{3,10},{10,... | collective-permute-start | bytes 196616 | tf_op jit(solution)/shard_map/ppermute | solution.py:15
  201.4 4.1 %collective-permute-start.10 = (f32[64,18,1]{0,1,2:T(8,128)S(1)}, f32[64,18,1]{0,1,2:T(8,128)S(1)}, u32[]{:S(2)}, u32[]{:S(2)}) collective-permute-start(f32[64,18,1]{0,1,2:T(8,128)S(1)} %get-tuple-element.21), channel_id=1, source_target_pairs={{0,2},{2,4},{4,6},{1,3},{3,5},{5,7},{8,10},{10,12},{12,14},{9,11},... | collective-permute-start | bytes 13832 | tf_op jit(solution)/shard_map/ppermute | solution.py:15
  204.3 3.7 %collective-permute-start.11 = (f32[64,18,1]{0,1,2:T(8,128)S(1)}, f32[64,18,1]{0,1,2:T(8,128)S(1)}, u32[]{:S(2)}, u32[]{:S(2)}) collective-permute-start(f32[64,18,1]{0,1,2:T(8,128)S(1)} %get-tuple-element.22), channel_id=1, source_target_pairs={{2,0},{4,2},{6,4},{3,1},{5,3},{7,5},{10,8},{12,10},{14,12},{11,9},... | collective-permute-start | bytes 13832 | tf_op jit(solution)/shard_map/ppermute | solution.py:18
  217.5 6.5 %collective-permute-start.13 = (f32[64,1,256]{2,0,1:T(8,128)S(1)}, f32[64,1,256]{2,0,1:T(8,128)S(1)}, u32[]{:S(2)}, u32[]{:S(2)}) collective-permute-start(f32[64,1,256]{2,0,1:T(8,128)S(1)} %copy.154), channel_id=1, source_target_pairs={{1,0},{8,1},{9,8},{16,9},{17,16},{24,17},{25,24},{3,2},{10,3},{11,... | collective-permute-start | bytes 196616 | tf_op jit(solution)/shard_map/ppermute | solution.py:18
  218.9 6.8 %collective-permute-start.12 = (f32[64,1,256]{2,0,1:T(8,128)S(1)}, f32[64,1,256]{2,0,1:T(8,128)S(1)}, u32[]{:S(2)}, u32[]{:S(2)}) collective-permute-start(f32[64,1,256]{2,0,1:T(8,128)S(1)} %copy.152), channel_id=1, source_target_pairs={{0,1},{1,8},{8,9},{9,16},{16,17},{17,24},{24,25},{2,3},{3,10},{10,... | collective-permute-start | bytes 196616 | tf_op jit(solution)/shard_map/ppermute | solution.py:15
  225.8 4.9 %collective-permute-start.14 = (f32[64,18,1]{0,1,2:T(8,128)S(1)}, f32[64,18,1]{0,1,2:T(8,128)S(1)}, u32[]{:S(2)}, u32[]{:S(2)}) collective-permute-start(f32[64,18,1]{0,1,2:T(8,128)S(1)} %get-tuple-element.19), channel_id=1, source_target_pairs={{0,2},{2,4},{4,6},{1,3},{3,5},{5,7},{8,10},{10,12},{12,14},{9,11},... | collective-permute-start | bytes 13832 | tf_op jit(solution)/shard_map/ppermute | solution.py:15
  229.4 3.4 %collective-permute-start.15 = (f32[64,18,1]{0,1,2:T(8,128)S(1)}, f32[64,18,1]{0,1,2:T(8,128)S(1)}, u32[]{:S(2)}, u32[]{:S(2)}) collective-permute-start(f32[64,18,1]{0,1,2:T(8,128)S(1)} %get-tuple-element.20), channel_id=1, source_target_pairs={{2,0},{4,2},{6,4},{3,1},{5,3},{7,5},{10,8},{12,10},{14,12},{11,9},... | collective-permute-start | bytes 13832 | tf_op jit(solution)/shard_map/ppermute | solution.py:18
Sparse Core Ops, SparseCore 0:
  26.6 91.6 all-reduce.2
  130.8 31.6 reduce-scatter.1
  241.6 38.3 all-gather.1
where the time goes:
time: 292 us; the launch traced here: 291 us
  waiting for transfers between devices  154 us (53%)
  starting transfers between devices  41.8 us (14%)
  matrix products  33 us (11%)
  other arithmetic  23.7 us (8%)
  between operations  14.2 us (5%)
  local copies, waits for them, and re-layouts  14.1 us (5%)
  blocking collectives  10.2 us (3%)
    psum x1, waiting for transfers between devices, shards(): chan_top, pixel_gram = lax.psum((chan_top, pixel_gram), ('row', 'col'))  91.5 us
    all_gather x1, waiting for transfers between devices, shards(): smoothed_factor = lax.all_gather(field, 'ch', axis=1, tiled=True)  38.5 us
    ppermute x8, starting transfers between devices, padded_2(): lax.ppermute(lax.slice_in_dim(block, block.shape[dim] - width, None, axis...  31 us
    div x3, other arithmetic, smooth_once(): return combined / (1.0 + weights[0] + weights[1] + weights[2] + weights[3])  23.6 us
    reduce_scatter x1, waiting for transfers between devices, shards(): lax.psum_scatter(part_top, 'ch', scatter_dimension=1, tiled=True)  13.5 us
    dot_general x1, matrix products, shards(): lax.dot_general(flat_pixel, flat_data, contraction, precision=precise, pr...  12.2 us
    dot_general x1, matrix products, shards(): jnp.dot(new_channel, flat_data, precision=precise, preferred_element_type...  11.4 us
    ppermute x8, starting transfers between devices, padded_2(): lax.ppermute(lax.slice_in_dim(block, 0, width, axis=dim), axis, backward)  10.5 us
  transfers between devices with their start and end apart: 19, of which 11 were waited for; matrix products, arithmetic and copies ran while one was open for 1% of the time, Pallas kernels for 0%

commit v1 on v0

--- a/solution.py
+++ b/solution.py
@@ -91,7 +91,7 @@
     for iteration in range(SMOOTH):
         padded = padded_2(field, ((("row", "ch"), 1), ("col", 2)), 1)
         field = smooth_once(padded, field, weights)
-    smoothed_factor = lax.all_gather(field, "ch", axis=1, tiled=True)
+    smoothed_factor = jnp.concatenate(lax.all_gather(field, "ch"), axis=1)
     return (smoothed_factor, new_channel)
 
 

time: 292 us -> 279 us (0.955)
  other arithmetic: 23.7 us -> 14.7 us
  waiting for transfers between devices: 154 us -> 161 us
  local copies, waits for them, and re-layouts: 14.1 us -> 8.37 us
  starting transfers between devices: 41.8 us -> 36.6 us
    ppermute x8, waiting for transfers between devices: 5.83 us -> 19.3 us  [padded_2(): lax.ppermute(lax.slice_in_dim(block, 0, width, axis=dim), axis, backward)]
    div x3, other arithmetic: 23.6 us -> 14.5 us  [smooth_once(): return combined / (1.0 + weights[0] + weights[1] + weights[2] + weights[3])]
    ppermute x8, starting transfers between devices: 31 us -> 26 us  [padded_2(): lax.ppermute(lax.slice_in_dim(block, block.shape[dim] - width, None, axis...]
    all_gather x1, waiting for transfers between devices: 38.5 us -> 33.8 us  [shards(): smoothed_factor = jnp.concatenate(lax.all_gather(field, 'ch'), axis=1)]
    unnamed x17 -> x9, local copies, waits for them, and re-layouts: 5.77 us -> 1.3 us
    reshape x0 -> x1, local copies, waits for them, and re-layouts: none -> 3.15 us  [shards(): smoothed_factor = jnp.concatenate(lax.all_gather(field, 'ch'), axis=1)]
  transfers between devices with their start and end apart: 19 -> 19, of which waited for: 11 -> 12; matrix products, arithmetic and copies ran while one was open for 1% -> 0% of each run, Pallas kernels for 0% -> 0%
where the time goes in v1:
time: 279 us; the launch traced here: 278 us
  waiting for transfers between devices  161 us (58%)
  starting transfers between devices  36.6 us (13%)
  matrix products  33 us (12%)
  other arithmetic  14.7 us (5%)
  between operations  14.1 us (5%)
  blocking collectives  10.2 us (4%)
  local copies, waits for them, and re-layouts  8.37 us (3%)
    psum x1, waiting for transfers between devices, shards(): chan_top, pixel_gram = lax.psum((chan_top, pixel_gram), ('row', 'col'))  91.5 us
    all_gather x1, waiting for transfers between devices, shards(): smoothed_factor = jnp.concatenate(lax.all_gather(field, 'ch'), axis=1)  33.8 us
    ppermute x8, starting transfers between devices, padded_2(): lax.ppermute(lax.slice_in_dim(block, block.shape[dim] - width, None, axis...  26 us
    ppermute x8, waiting for transfers between devices, padded_2(): lax.ppermute(lax.slice_in_dim(block, 0, width, axis=dim), axis, backward)  19.3 us
    div x3, other arithmetic, smooth_once(): return combined / (1.0 + weights[0] + weights[1] + weights[2] + weights[3])  14.5 us
    reduce_scatter x1, waiting for transfers between devices, shards(): lax.psum_scatter(part_top, 'ch', scatter_dimension=1, tiled=True)  13.5 us
    dot_general x1, matrix products, shards(): lax.dot_general(flat_pixel, flat_data, contraction, precision=precise, pr...  12.2 us
    dot_general x1, matrix products, shards(): jnp.dot(new_channel, flat_data, precision=precise, preferred_element_type...  11.4 us
  transfers between devices with their start and end apart: 19, of which 12 were waited for; matrix products, arithmetic and copies ran while one was open for 0% of the time, Pallas kernels for 0%

profile of v1, /device:TPU:0, one launch (start us, length us, event | category | flops | bytes accessed | tf_op | source)
XLA Modules:
  0.0 278.1 jit_solution(4968628495983692188)
XLA Ops:
  7.2 7.0 %fusion.42 = f32[64,64]{1,0:T(8,128)} fusion(f32[64,32,256]{2,1,0:T(8,128)} %param.5), kind=kOutput, calls=%fused_computation.64 | convolution fusion | flops 402653184 | bytes 2113536 | tf_op jit(solution)/shard_map/dot_general | solution.py:61
  14.2 12.2 %fusion.36 = f32[64,192]{1,0:T(8,128)} fusion(f32[192,32,256]{2,1,0:T(8,128)} %param.4, f32[64,32,256]{2,1,0:T(8,128)S(1)} %copy-done), kind=kOutput, calls=%fused_computation.61 | convolution fusion | flops 1207959552 | bytes 8437760 | tf_op jit(solution)/shard_map/dot_general | solution.py:58
  26.5 0.2 reduce-scatter.2.cloned.1.call-start
  26.7 91.5 %all-reduce.3.cloned.1.call-done = (f32[64,64]{1,0:T(8,128)}, f32[64,192]{1,0:T(8,128)}) async-done(((f32[64,64]{1,0:T(8,128)}, f32[64,192]{1,0:T(8,128)}), (f32[64,64]{1,0:T(8,128)}, f32[64,192]{1,0:T(8,128)})) %all-reduce.3.cloned.1.call-update) | async-done | bytes 65552 | tf_op jit(solution)/shard_map/psum | solution.py:64
  118.2 1.1 fusion.41
  119.3 11.4 %fusion = f32[64,32,256]{2,0,1:T(8,128)} fusion(f32[64,192]{1,0:T(8,128)S(1)} %fusion.41, f32[24,8,32,256]{3,2,1,0:T(8,128)} %bitcast.33), kind=kOutput, calls=%fused_computation | convolution fusion | flops 1207959552 | bytes 8437760 | tf_op jit(solution)/shard_map/dot_general | solution.py:75
  130.8 0.7 copy-done.2
  131.5 1.3 collective-permute-start.2
  132.8 4.5 %collective-permute-start = (s32[1,256]{1,0:T(1,128)S(1)}, s32[1,256]{1,0:T(1,128)S(1)}, u32[]{:S(2)}, u32[]{:S(2)}) collective-permute-start(s32[1,256]{1,0:T(1,128)S(1)} %get-tuple-element.24), channel_id=1, source_target_pairs={{0,1},{1,8},{8,9},{9,16},{16,17},{17,24},{24,25},{2,3},{3,10},{10,... | collective-permute-start | bytes 3080 | tf_op jit(solution)/shard_map/ppermute | solution.py:15
  137.3 0.1 constant_dynamic-slice_fusion
  137.4 0.6 copy.31
  138.0 0.6 collective-permute-done
  138.6 0.2 fusion.55
  138.8 10.2 %psum.23 = f32[64,64]{1,0:T(8,128)S(1)} all-reduce(f32[64,64]{1,0:T(8,128)S(1)} %fusion.55), channel_id=1, replica_groups=mesh['row'=4,'col'=4,'ch'=2] {'ch'}, use_global_device_ids=true, to_apply=%region_3.0 | all-reduce | flops 4096 | bytes 32768 | tf_op jit(solution)/shard_map/psum | solution.py:85
  149.0 13.5 %reduce-scatter.2.cloned.1.call-done = f32[64,16,256]{2,0,1:T(8,128)} async-done(((f32[64,32,256]{2,0,1:T(8,128)}), f32[64,16,256]{2,0,1:T(8,128)}) %reduce-scatter.2.cloned.1.call-update) | async-done | bytes 1048592 | tf_op jit(solution)/shard_map/reduce_scatter | solution.py:84
  162.5 1.3 copy.30
  163.8 1.1 fusion.5
  165.0 0.6 copy.28
  165.6 2.3 collective-permute-start.1
  167.9 1.3 collective-permute-start.3
  169.2 0.1 fusion.53
  169.3 1.3 collective-permute-start.6
  170.6 3.0 %collective-permute-start.4 = (s32[18,1]{1,0:T(8,128)S(1)}, s32[18,1]{1,0:T(8,128)S(1)}, u32[]{:S(2)}, u32[]{:S(2)}) collective-permute-start(s32[18,1]{1,0:T(8,128)S(1)} %get-tuple-element.22), channel_id=1, source_target_pairs={{0,2},{2,4},{4,6},{1,3},{3,5},{5,7},{8,10},{10,12},{12,14},{9,11},... | collective-permute-start | bytes 224 | tf_op jit(solution)/shard_map/ppermute | solution.py:15
  173.6 1.8 collective-permute-done.3
  175.5 1.4 collective-permute-start.5
  176.9 1.3 collective-permute-start.7
  178.2 0.1 add_add_fusion
  178.3 3.3 %collective-permute-done.7 = f32[64,18,1]{0,2,1:T(1,128)S(1)} collective-permute-done((f32[64,18,1]{0,2,1:T(1,128)S(1)}, f32[64,18,1]{0,2,1:T(1,128)S(1)}, u32[]{:S(2)}, u32[]{:S(2)}) %collective-permute-start.7) | collective-permute-done | bytes 4640 | tf_op jit(solution)/shard_map/ppermute | solution.py:18
  181.6 4.8 %fusion.26 = f32[64,16,256]{0,2,1:T(8,128)S(1)} fusion(f32[64,18,1]{0,2,1:T(1,128)S(1)} %collective-permute-done.7, f32[64,1,256]{0,2,1:T(8,128)S(1)} %collective-permute-done.3, f32[64,16,256]{0,2,1:T(8,128)S(1)} %bitcast.36, f32[64,1,256]{0,2,1:T(8,128)S(1)} %collective-permute-done.1, f32[64,18,1]{0,2,1:T(1,128)S(1)} %collective-permute-done.5, ...), kind=kLoop, calls=%fused_computation.44 | loop fusion | flops 4456448 | bytes 2319360 | tf_op jit(solution)/shard_map/div | solution.py:38
  186.4 4.7 %collective-permute-start.8 = (f32[64,1,256]{0,2,1:T(8,128)S(1)}, f32[64,1,256]{0,2,1:T(8,128)S(1)}, u32[]{:S(2)}, u32[]{:S(2)}) collective-permute-start(f32[64,1,256]{0,2,1:T(8,128)S(1)} %get-tuple-element.17), channel_id=1, source_target_pairs={{0,1},{1,8},{8,9},{9,16},{16,17},{17,24},{24,25},{2,3},{3,10},{10,... | collective-permute-start | bytes 196616 | tf_op jit(solution)/shard_map/ppermute | solution.py:15
  191.1 1.3 collective-permute-start.9
  192.4 1.2 collective-permute-done.8
  193.6 4.6 %collective-permute-done.9 = f32[64,1,256]{0,2,1:T(8,128)S(1)} collective-permute-done((f32[64,1,256]{0,2,1:T(8,128)S(1)}, f32[64,1,256]{0,2,1:T(8,128)S(1)}, u32[]{:S(2)}, u32[]{:S(2)}) %collective-permute-start.9) | collective-permute-done | bytes 65568 | tf_op jit(solution)/shard_map/ppermute | solution.py:18
  198.3 2.9 %collective-permute-start.10 = (f32[64,18,1]{0,2,1:T(1,128)S(1)}, f32[64,18,1]{0,2,1:T(1,128)S(1)}, u32[]{:S(2)}, u32[]{:S(2)}) collective-permute-start(f32[64,18,1]{0,2,1:T(1,128)S(1)} %get-tuple-element.11), channel_id=1, source_target_pairs={{0,2},{2,4},{4,6},{1,3},{3,5},{5,7},{8,10},{10,12},{12,14},{9,11},... | collective-permute-start | bytes 13832 | tf_op jit(solution)/shard_map/ppermute | solution.py:15
  201.2 1.3 collective-permute-start.11
  202.5 2.5 collective-permute-done.11
  204.9 4.8 %fusion.17 = f32[64,16,256]{0,2,1:T(8,128)S(1)} fusion(f32[64,18,1]{0,2,1:T(1,128)S(1)} %collective-permute-done.11, f32[64,1,256]{0,2,1:T(8,128)S(1)} %collective-permute-done.9, f32[64,16,256]{0,2,1:T(8,128)S(1)} %fusion.26, f32[64,1,256]{0,2,1:T(8,128)S(1)} %collective-permute-done.8, f32[64,18,1]{0,2,1:T(1,128)S(1)} %collective-permute-done.10, ...), kind=kLoop, calls=%fused_computation.27 | loop fusion | flops 4456448 | bytes 2319360 | tf_op jit(solution)/shard_map/div | solution.py:38
  209.8 4.3 %collective-permute-start.12 = (f32[64,1,256]{0,2,1:T(8,128)S(1)}, f32[64,1,256]{0,2,1:T(8,128)S(1)}, u32[]{:S(2)}, u32[]{:S(2)}) collective-permute-start(f32[64,1,256]{0,2,1:T(8,128)S(1)} %get-tuple-element.15), channel_id=1, source_target_pairs={{0,1},{1,8},{8,9},{9,16},{16,17},{17,24},{24,25},{2,3},{3,10},{10,... | collective-permute-start | bytes 196616 | tf_op jit(solution)/shard_map/ppermute | solution.py:15
  214.1 1.3 collective-permute-start.13
  215.4 1.2 collective-permute-done.12
  216.6 4.6 %collective-permute-done.13 = f32[64,1,256]{0,2,1:T(8,128)S(1)} collective-permute-done((f32[64,1,256]{0,2,1:T(8,128)S(1)}, f32[64,1,256]{0,2,1:T(8,128)S(1)}, u32[]{:S(2)}, u32[]{:S(2)}) %collective-permute-start.13) | collective-permute-done | bytes 65568 | tf_op jit(solution)/shard_map/ppermute | solution.py:18
  221.3 2.9 %collective-permute-start.14 = (f32[64,18,1]{0,2,1:T(1,128)S(1)}, f32[64,18,1]{0,2,1:T(1,128)S(1)}, u32[]{:S(2)}, u32[]{:S(2)}) collective-permute-start(f32[64,18,1]{0,2,1:T(1,128)S(1)} %get-tuple-element.9), channel_id=1, source_target_pairs={{0,2},{2,4},{4,6},{1,3},{3,5},{5,7},{8,10},{10,12},{12,14},{9,11},... | collective-permute-start | bytes 13832 | tf_op jit(solution)/shard_map/ppermute | solution.py:15
  224.2 1.3 collective-permute-start.15
  225.5 2.5 collective-permute-done.15
  228.0 4.8 %fusion.8 = f32[64,16,256]{0,2,1:T(8,128)S(1)} fusion(f32[64,18,1]{0,2,1:T(1,128)S(1)} %collective-permute-done.15, f32[64,1,256]{0,2,1:T(8,128)S(1)} %collective-permute-done.13, f32[64,16,256]{0,2,1:T(8,128)S(1)} %fusion.17, f32[64,1,256]{0,2,1:T(8,128)S(1)} %collective-permute-done.12, f32[64,18,1]{0,2,1:T(1,128)S(1)} %collective-permute-done.14, ...), kind=kLoop, calls=%fused_computation.10 | loop fusion | flops 4456448 | bytes 2319360 | tf_op jit(solution)/shard_map/div | solution.py:38
  232.8 1.8 copy.26
  234.6 33.8 %all-gather.3.cloned.1.call-done = f32[128,16,256]{2,1,0:T(8,128)} async-done(((f32[64,16,256]{2,1,0:T(8,128)}), f32[128,16,256]{2,1,0:T(8,128)}) %all-gather.3.cloned.1.call-update) | async-done | bytes 2097168 | tf_op jit(solution)/shard_map/all_gather | solution.py:94
  268.4 3.2 %copy.27 = f32[64,2,16,256]{3,2,1,0:T(8,128)} copy(f32[64,2,16,256]{3,2,0,1:T(8,128)} %bitcast.38) | data formatting | bytes 4194304 | tf_op jit(solution)/shard_map/reshape | solution.py:94
  (28 shorter events, 0.3 us)
Async XLA Ops:
  7.2 7.1 %copy-start = (f32[64,32,256]{2,1,0:T(8,128)S(1)}, f32[64,32,256]{2,1,0:T(8,128)}, u32[]{:S(2)}) copy-start(f32[64,32,256]{2,1,0:T(8,128)} %param.5) | copy-start | bytes 6291460
  7.2 111.1 %all-reduce.3.cloned.1.call-start = ((), (), s32[]{:S(2)}) async-start(), calls=%async_computation.3 | async-start | bytes 196608 | tf_op jit(solution)/shard_map/psum | solution.py:64
  14.2 104.0 %copy-start.3 = (f32[64,192]{1,0:T(8,128)S(1)}, f32[64,192]{1,0:T(8,128)}, u32[]{:S(2)}) copy-start(f32[64,192]{1,0:T(8,128)} %param.6) | copy-start | bytes 147460
  26.5 136.1 %reduce-scatter.2.cloned.1.call-start = ((), (), s32[]{:S(2)}) async-start(), calls=%async_computation.1 | async-start | bytes 3145728 | tf_op jit(solution)/shard_map/reduce_scatter | solution.py:84
  119.3 19.3 %copy-start.1 = (f32[64,192]{1,0:T(8,128)}, f32[64,192]{1,0:T(8,128)S(1)}, u32[]{:S(2)}) copy-start(f32[64,192]{1,0:T(8,128)S(1)} %fusion.41) | copy-start | bytes 147460
  130.7 0.8 copy-start.2
  130.7 137.7 %all-gather.3.cloned.1.call-start = ((), (), s32[]{:S(2)}) async-start(), calls=%async_computation.2 | async-start | bytes 3145728 | tf_op jit(solution)/shard_map/all_gather | solution.py:94
  131.5 6.6 %collective-permute-start.2 = (s32[1,256]{1,0:T(1,128)S(1)}, s32[1,256]{1,0:T(1,128)S(1)}, u32[]{:S(2)}, u32[]{:S(2)}) collective-permute-start(s32[1,256]{1,0:T(1,128)S(1)} %get-tuple-element.23), channel_id=1, source_target_pairs={{1,0},{8,1},{9,8},{16,9},{17,16},{24,17},{25,24},{3,2},{10,3},{11,... | collective-permute-start | bytes 3080 | tf_op jit(solution)/shard_map/ppermute | solution.py:18
  132.8 5.8 %collective-permute-start = (s32[1,256]{1,0:T(1,128)S(1)}, s32[1,256]{1,0:T(1,128)S(1)}, u32[]{:S(2)}, u32[]{:S(2)}) collective-permute-start(s32[1,256]{1,0:T(1,128)S(1)} %get-tuple-element.24), channel_id=1, source_target_pairs={{0,1},{1,8},{8,9},{9,16},{16,17},{17,24},{24,25},{2,3},{3,10},{10,... | collective-permute-start | bytes 3080 | tf_op jit(solution)/shard_map/ppermute | solution.py:15
  165.6 8.0 %collective-permute-start.1 = (f32[64,1,256]{0,2,1:T(8,128)S(1)}, f32[64,1,256]{0,2,1:T(8,128)S(1)}, u32[]{:S(2)}, u32[]{:S(2)}) collective-permute-start(f32[64,1,256]{0,2,1:T(8,128)S(1)} %get-tuple-element.19), channel_id=1, source_target_pairs={{0,1},{1,8},{8,9},{9,16},{16,17},{17,24},{24,25},{2,3},{3,10},{10,... | collective-permute-start | bytes 196616 | tf_op jit(solution)/shard_map/ppermute | solution.py:15
  167.9 7.6 %collective-permute-start.3 = (f32[64,1,256]{0,2,1:T(8,128)S(1)}, f32[64,1,256]{0,2,1:T(8,128)S(1)}, u32[]{:S(2)}, u32[]{:S(2)}) collective-permute-start(f32[64,1,256]{0,2,1:T(8,128)S(1)} %get-tuple-element.20), channel_id=1, source_target_pairs={{1,0},{8,1},{9,8},{16,9},{17,16},{24,17},{25,24},{3,2},{10,3},{11,... | collective-permute-start | bytes 196616 | tf_op jit(solution)/shard_map/ppermute | solution.py:18
  169.3 8.9 %collective-permute-start.6 = (s32[18,1]{1,0:T(8,128)S(1)}, s32[18,1]{1,0:T(8,128)S(1)}, u32[]{:S(2)}, u32[]{:S(2)}) collective-permute-start(s32[18,1]{1,0:T(8,128)S(1)} %get-tuple-element.21), channel_id=1, source_target_pairs={{2,0},{4,2},{6,4},{3,1},{5,3},{7,5},{10,8},{12,10},{14,12},{11,9},... | collective-permute-start | bytes 224 | tf_op jit(solution)/shard_map/ppermute | solution.py:18
  170.6 7.6 %collective-permute-start.4 = (s32[18,1]{1,0:T(8,128)S(1)}, s32[18,1]{1,0:T(8,128)S(1)}, u32[]{:S(2)}, u32[]{:S(2)}) collective-permute-start(s32[18,1]{1,0:T(8,128)S(1)} %get-tuple-element.22), channel_id=1, source_target_pairs={{0,2},{2,4},{4,6},{1,3},{3,5},{5,7},{8,10},{10,12},{12,14},{9,11},... | collective-permute-start | bytes 224 | tf_op jit(solution)/shard_map/ppermute | solution.py:15
  175.5 2.8 %collective-permute-start.5 = (f32[64,18,1]{0,2,1:T(1,128)S(1)}, f32[64,18,1]{0,2,1:T(1,128)S(1)}, u32[]{:S(2)}, u32[]{:S(2)}) collective-permute-start(f32[64,18,1]{0,2,1:T(1,128)S(1)} %get-tuple-element.13), channel_id=1, source_target_pairs={{0,2},{2,4},{4,6},{1,3},{3,5},{5,7},{8,10},{10,12},{12,14},{9,11},... | collective-permute-start | bytes 13832 | tf_op jit(solution)/shard_map/ppermute | solution.py:15
  176.9 4.7 %collective-permute-start.7 = (f32[64,18,1]{0,2,1:T(1,128)S(1)}, f32[64,18,1]{0,2,1:T(1,128)S(1)}, u32[]{:S(2)}, u32[]{:S(2)}) collective-permute-start(f32[64,18,1]{0,2,1:T(1,128)S(1)} %get-tuple-element.14), channel_id=1, source_target_pairs={{2,0},{4,2},{6,4},{3,1},{5,3},{7,5},{10,8},{12,10},{14,12},{11,9},... | collective-permute-start | bytes 13832 | tf_op jit(solution)/shard_map/ppermute | solution.py:18
  186.4 7.2 %collective-permute-start.8 = (f32[64,1,256]{0,2,1:T(8,128)S(1)}, f32[64,1,256]{0,2,1:T(8,128)S(1)}, u32[]{:S(2)}, u32[]{:S(2)}) collective-permute-start(f32[64,1,256]{0,2,1:T(8,128)S(1)} %get-tuple-element.17), channel_id=1, source_target_pairs={{0,1},{1,8},{8,9},{9,16},{16,17},{17,24},{24,25},{2,3},{3,10},{10,... | collective-permute-start | bytes 196616 | tf_op jit(solution)/shard_map/ppermute | solution.py:15
  191.1 7.1 %collective-permute-start.9 = (f32[64,1,256]{0,2,1:T(8,128)S(1)}, f32[64,1,256]{0,2,1:T(8,128)S(1)}, u32[]{:S(2)}, u32[]{:S(2)}) collective-permute-start(f32[64,1,256]{0,2,1:T(8,128)S(1)} %get-tuple-element.18), channel_id=1, source_target_pairs={{1,0},{8,1},{9,8},{16,9},{17,16},{24,17},{25,24},{3,2},{10,3},{11,... | collective-permute-start | bytes 196616 | tf_op jit(solution)/shard_map/ppermute | solution.py:18
  198.3 4.2 %collective-permute-start.10 = (f32[64,18,1]{0,2,1:T(1,128)S(1)}, f32[64,18,1]{0,2,1:T(1,128)S(1)}, u32[]{:S(2)}, u32[]{:S(2)}) collective-permute-start(f32[64,18,1]{0,2,1:T(1,128)S(1)} %get-tuple-element.11), channel_id=1, source_target_pairs={{0,2},{2,4},{4,6},{1,3},{3,5},{5,7},{8,10},{10,12},{12,14},{9,11},... | collective-permute-start | bytes 13832 | tf_op jit(solution)/shard_map/ppermute | solution.py:15
  201.2 3.8 %collective-permute-start.11 = (f32[64,18,1]{0,2,1:T(1,128)S(1)}, f32[64,18,1]{0,2,1:T(1,128)S(1)}, u32[]{:S(2)}, u32[]{:S(2)}) collective-permute-start(f32[64,18,1]{0,2,1:T(1,128)S(1)} %get-tuple-element.12), channel_id=1, source_target_pairs={{2,0},{4,2},{6,4},{3,1},{5,3},{7,5},{10,8},{12,10},{14,12},{11,9},... | collective-permute-start | bytes 13832 | tf_op jit(solution)/shard_map/ppermute | solution.py:18
  209.8 6.8 %collective-permute-start.12 = (f32[64,1,256]{0,2,1:T(8,128)S(1)}, f32[64,1,256]{0,2,1:T(8,128)S(1)}, u32[]{:S(2)}, u32[]{:S(2)}) collective-permute-start(f32[64,1,256]{0,2,1:T(8,128)S(1)} %get-tuple-element.15), channel_id=1, source_target_pairs={{0,1},{1,8},{8,9},{9,16},{16,17},{17,24},{24,25},{2,3},{3,10},{10,... | collective-permute-start | bytes 196616 | tf_op jit(solution)/shard_map/ppermute | solution.py:15
  214.1 7.1 %collective-permute-start.13 = (f32[64,1,256]{0,2,1:T(8,128)S(1)}, f32[64,1,256]{0,2,1:T(8,128)S(1)}, u32[]{:S(2)}, u32[]{:S(2)}) collective-permute-start(f32[64,1,256]{0,2,1:T(8,128)S(1)} %get-tuple-element.16), channel_id=1, source_target_pairs={{1,0},{8,1},{9,8},{16,9},{17,16},{24,17},{25,24},{3,2},{10,3},{11,... | collective-permute-start | bytes 196616 | tf_op jit(solution)/shard_map/ppermute | solution.py:18
  221.3 4.2 %collective-permute-start.14 = (f32[64,18,1]{0,2,1:T(1,128)S(1)}, f32[64,18,1]{0,2,1:T(1,128)S(1)}, u32[]{:S(2)}, u32[]{:S(2)}) collective-permute-start(f32[64,18,1]{0,2,1:T(1,128)S(1)} %get-tuple-element.9), channel_id=1, source_target_pairs={{0,2},{2,4},{4,6},{1,3},{3,5},{5,7},{8,10},{10,12},{12,14},{9,11},... | collective-permute-start | bytes 13832 | tf_op jit(solution)/shard_map/ppermute | solution.py:15
  224.2 3.8 %collective-permute-start.15 = (f32[64,18,1]{0,2,1:T(1,128)S(1)}, f32[64,18,1]{0,2,1:T(1,128)S(1)}, u32[]{:S(2)}, u32[]{:S(2)}) collective-permute-start(f32[64,18,1]{0,2,1:T(1,128)S(1)} %get-tuple-element.10), channel_id=1, source_target_pairs={{2,0},{4,2},{6,4},{3,1},{5,3},{7,5},{10,8},{12,10},{14,12},{11,9},... | collective-permute-start | bytes 13832 | tf_op jit(solution)/shard_map/ppermute | solution.py:18
Sparse Core Ops, SparseCore 0:
  26.6 91.6 all-reduce.2
  130.8 31.6 reduce-scatter.1
  234.7 33.6 all-gather.2
